TPU v7x, 256 devices: a whole 4x4x8 slice. The times are simulated.
256 devices in a mesh: freq: 16 (over x, z_hi), tile: 16 (over z_lo, y, core).
Axes of the slice: x: 4, y: 4, z: 8 (z_hi: 4, z_lo: 2; z = z_hi * 2 + z_lo), core: 2. Of those that a mesh axis runs over, the one named last changes fastest.
Arguments:
- sky_cube: float32 [256, 256, 128], P(('freq', 'tile')), may hold values from -6 to 6
- kernel_one: bfloat16 [8, 1, 3, 3, 3], replicated, may hold values from -1.25 to 1.25
- bias_one: float32 [8], replicated, may hold values from -2 to 2
- kernel_two: bfloat16 [8, 8, 3, 3, 3], replicated, may hold values from -0.4375 to 0.4375
- bias_two: float32 [8], replicated, may hold values from -2 to 2
- kernel_three: bfloat16 [16, 8, 3, 3, 3], replicated, may hold values from -0.4375 to 0.4375
- bias_three: float32 [16], replicated, may hold values from -2 to 2
Outputs:
- features: bfloat16 [16, 128, 128, 64], P(None, 'freq', 'tile')
All inputs are finite; a program needn't handle non-finite values.
Results may differ from a plain program's by a relative error of at most 0.0066.
Values may be sent and summed in bfloat16 or wider, within the bound.
A program may use at most 64 MiB of HBM per device.

v0:
```python
import jax
import jax.numpy as jnp
from jax import lax
from jax.sharding import PartitionSpec as P


def extended_2(cells, sides, width):
    for axis, dim in sides:
        count = lax.axis_size(axis)
        ends = count - 1
        head = lax.slice_in_dim(cells, 0, width, axis=dim)
        tail = lax.slice_in_dim(cells, cells.shape[dim] - width, cells.shape[dim], axis=dim)
        cells = jnp.concatenate(
            [
                lax.ppermute(tail, axis, [(i, (i + 1) % count) for i in range(ends)]),
                cells,
                lax.ppermute(head, axis, [((i + 1) % count, i) for i in range(ends)]),
            ],
            axis=dim,
        )
    return cells


def shortened(shard):

    def short(part):
        return part.astype(jnp.bfloat16) if part.dtype == jnp.float32 else part

    return jax.tree.map(short, shard)


def from_behind(shard, axis, by):
    devices = lax.axis_size(axis)
    pairs = [(i, i + by) for i in range(devices) if 0 <= i + by < devices]
    return lax.ppermute(shard, axis, pairs)


def leaky_relu(values):
    return jnp.maximum(values, 0.1 * values)


def conv_layer(volume, kernel, bias_term):
    depth = volume.shape[1] - 2
    blocks = []
    for begin_at in range(0, depth, 4):
        count = min(4, depth - begin_at)
        section = volume[:, begin_at : begin_at + count + 2]
        values = lax.conv_general_dilated(
            section[None],
            kernel,
            (1, 1, 1),
            ((0, 0), (0, 0), (1, 1)),
            dimension_numbers=("NCDHW", "OIDHW", "NCDHW"),
            preferred_element_type=jnp.float32,
        )[0]
        values = leaky_relu(values + bias_term[:, None, None, None])
        blocks.append(values.astype(jnp.bfloat16))
    return jnp.concatenate(blocks, axis=1)


def body(sky_cube, kernel_one, bias_one, kernel_two, bias_two, kernel_three, bias_three):
    slab = lax.all_to_all(
        sky_cube.astype(jnp.bfloat16), "tile", split_axis=1, concat_axis=0, tiled=True
    )
    widened = extended_2(slab, (("freq", 0), ("tile", 1)), 1)
    layer_one = conv_layer(widened[None], kernel_one, bias_one)
    widened = extended_2(layer_one, (("freq", 1), ("tile", 2)), 1)
    layer_two = conv_layer(widened, kernel_two, bias_two)
    lower_rows = from_behind(shortened(layer_two[:, :, -1:, :]), "tile", 1)
    extended = jnp.concatenate([lower_rows, layer_two], axis=2)
    lower_planes = from_behind(shortened(extended[:, -1:]), "freq", 1)
    extended = jnp.concatenate([lower_planes, extended], axis=1)
    values = lax.conv_general_dilated(
        extended[None],
        kernel_three,
        (2, 2, 2),
        ((0, 0), (0, 0), (1, 1)),
        dimension_numbers=("NCDHW", "OIDHW", "NCDHW"),
        preferred_element_type=jnp.float32,
    )[0]
    return leaky_relu(values + bias_three[:, None, None, None]).astype(jnp.bfloat16)


def solution(mesh):
    return jax.shard_map(
        body,
        mesh=mesh,
        in_specs=(P(("freq", "tile"), None, None), P(), P(), P(), P(), P(), P()),
        out_specs=P(None, "freq", "tile", None),
        check_vma=False,
    )
```

profile of v0, /device:TPU:34, one launch (start us, length us, event | category | flops | bytes accessed | tf_op | source)
XLA Modules:
  0.0 293.2 jit_solution(5028507617221354503)
XLA Ops:
  2.6 10.6 %all_to_all.15 = bf16[16,2,1024]{2,1,0:T(2,128)(2,1)S(1)} all-to-all(bf16[16,2,1024]{2,1,0:T(2,128)(2,1)S(1)} %reshape.116), channel_id=1, replica_groups=mesh['freq'=16,'tile'=16] {'tile'}, dimensions={0} | all-to-all | bytes 131072 | tf_op jit(solution)/shard_map/all_to_all | solution.py:62
  13.3 5.2 %collective-permute-start = (bf16[1,16,128]{2,1,0:T(8,128)(2,1)S(1)}, bf16[1,16,128]{2,1,0:T(8,128)(2,1)S(1)}, u32[]{:S(2)}, u32[]{:S(2)}) collective-permute-start(bf16[1,16,128]{2,1,0:T(8,128)(2,1)S(1)} %slice_bitcast_fusion.16), channel_id=1, source_target_pairs={{0,16},{16,32},{32,48},{48,64},{64,80},{80,96},{96,112},{112,128},... | collective-permute-start | bytes 12296 | tf_op jit(solution)/shard_map/ppermute | solution.py:15
  18.5 4.0 %collective-permute-start.1 = (bf16[1,16,128]{2,1,0:T(8,128)(2,1)S(1)}, bf16[1,16,128]{2,1,0:T(8,128)(2,1)S(1)}, u32[]{:S(2)}, u32[]{:S(2)}) collective-permute-start(bf16[1,16,128]{2,1,0:T(8,128)(2,1)S(1)} %copy.172), channel_id=1, source_target_pairs={{16,0},{32,16},{48,32},{64,48},{80,64},{96,80},{112,96},{128,112},... | collective-permute-start | bytes 12296 | tf_op jit(solution)/shard_map/ppermute | solution.py:17
  27.5 5.8 %collective-permute-start.3 = (bf16[18,1,128]{2,1,0:T(2,128)(2,1)S(1)}, bf16[18,1,128]{2,1,0:T(2,128)(2,1)S(1)}, u32[]{:S(2)}, u32[]{:S(2)}) collective-permute-start(bf16[18,1,128]{2,1,0:T(2,128)(2,1)S(1)} %get-tuple-element.18), channel_id=1, source_target_pairs={{1,0},{2,1},{3,2},{4,3},{5,4},{6,5},{7,6},{8,7},{9,8},{10,9},{11,1... | collective-permute-start | bytes 13832 | tf_op jit(solution)/shard_map/ppermute | solution.py:17
  44.9 8.6 %broadcast_select_fusion.4 = f32[4,16,8,17,8]{4,2,3,1,0:T(8,128)} fusion(pred[8,17]{0,1:T(8,128)(4,1)S(1)} %copy-done.6, bf16[1,6,18,8,19]{3,0,4,2,1:T(2,128)(2,1)S(1)} %copy.151, bf16[8,1,3,3,3]{0,4,3,2,1:T(4,128)(2,1)S(1)} %copy-done.5), kind=kOutput, calls=%fused_computation.39 | convolution fusion | flops 3829760 | bytes 311928 | tf_op jit(solution)/shard_map/conv_general_dilated | solution.py:48
  53.6 8.7 %broadcast_select_fusion.5 = f32[4,16,8,17,8]{4,2,3,1,0:T(8,128)} fusion(pred[8,17]{0,1:T(8,128)(4,1)S(1)} %copy-done.6, bf16[1,6,18,8,19]{3,0,4,2,1:T(2,128)(2,1)S(1)} %copy.148, bf16[8,1,3,3,3]{0,4,3,2,1:T(4,128)(2,1)S(1)} %copy-done.5), kind=kOutput, calls=%fused_computation.40 | convolution fusion | flops 3829760 | bytes 311928 | tf_op jit(solution)/shard_map/conv_general_dilated | solution.py:48
  62.3 8.8 %broadcast_select_fusion.7 = f32[4,16,8,17,8]{4,2,3,1,0:T(8,128)} fusion(pred[8,17]{0,1:T(8,128)(4,1)S(1)} %copy-done.6, bf16[1,6,18,8,19]{3,0,4,2,1:T(2,128)(2,1)S(1)} %copy.142, bf16[8,1,3,3,3]{0,4,3,2,1:T(4,128)(2,1)S(1)} %copy-done.5), kind=kOutput, calls=%fused_computation.42 | convolution fusion | flops 3829760 | bytes 311928 | tf_op jit(solution)/shard_map/conv_general_dilated | solution.py:48
  71.0 5.4 %copy.144 = f32[4,16,8,17,8]{3,2,4,1,0:T(8,128)S(1)} copy(f32[4,16,8,17,8]{4,2,3,1,0:T(8,128)} %broadcast_select_fusion.7) | data formatting | bytes 557056 | tf_op jit(solution)/shard_map/conv_general_dilated | solution.py:48
  77.1 6.0 %collective-permute-start.4 = (bf16[8,1,16,128]{3,0,2,1:T(8,128)(2,1)S(1)}, bf16[8,1,16,128]{3,0,2,1:T(8,128)(2,1)S(1)}, u32[]{:S(2)}, u32[]{:S(2)}) collective-permute-start(bf16[8,1,16,128]{3,0,2,1:T(8,128)(2,1)S(1)} %slice.100), channel_id=1, source_target_pairs={{0,16},{16,32},{32,48},{48,64},{64,80},{80,96},{96,112},{112,128},... | collective-permute-start | bytes 98312 | tf_op jit(solution)/shard_map/ppermute | solution.py:15
  83.2 9.6 %broadcast_select_fusion.6 = f32[4,16,8,17,8]{4,2,3,1,0:T(8,128)} fusion(pred[8,17]{0,1:T(8,128)(4,1)S(1)} %copy-done.6, bf16[1,6,18,8,19]{3,0,4,2,1:T(2,128)(2,1)} %copy.145, bf16[8,1,3,3,3]{0,4,3,2,1:T(4,128)(2,1)S(1)} %copy-done.5), kind=kOutput, calls=%fused_computation.41 | convolution fusion | flops 3829760 | bytes 311928 | tf_op jit(solution)/shard_map/conv_general_dilated | solution.py:48
  92.7 5.2 %copy.153 = f32[4,16,8,17,8]{3,2,4,1,0:T(8,128)S(1)} copy(f32[4,16,8,17,8]{4,2,3,1,0:T(8,128)} %broadcast_select_fusion.4) | data formatting | bytes 557056 | tf_op jit(solution)/shard_map/conv_general_dilated | solution.py:48
  99.3 5.2 %copy.150 = f32[4,16,8,17,8]{3,2,4,1,0:T(8,128)S(1)} copy(f32[4,16,8,17,8]{4,2,3,1,0:T(8,128)} %broadcast_select_fusion.5) | data formatting | bytes 557056 | tf_op jit(solution)/shard_map/conv_general_dilated | solution.py:48
  105.9 5.2 %copy.147 = f32[4,16,8,17,8]{3,2,4,1,0:T(8,128)S(1)} copy(f32[4,16,8,17,8]{4,2,3,1,0:T(8,128)} %broadcast_select_fusion.6) | data formatting | bytes 557056 | tf_op jit(solution)/shard_map/conv_general_dilated | solution.py:48
  120.5 5.8 %collective-permute-start.7 = (bf16[8,18,1,128]{3,0,2,1:T(8,128)(2,1)S(1)}, bf16[8,18,1,128]{3,0,2,1:T(8,128)(2,1)S(1)}, u32[]{:S(2)}, u32[]{:S(2)}) collective-permute-start(bf16[8,18,1,128]{3,0,2,1:T(8,128)(2,1)S(1)} %get-tuple-element.12), channel_id=1, source_target_pairs={{1,0},{2,1},{3,2},{4,3},{5,4},{6,5},{7,6},{8,7},{9,8},{10,9},{11,1... | collective-permute-start | bytes 110600 | tf_op jit(solution)/shard_map/ppermute | solution.py:17
  137.1 6.7 %copy.155 = bf16[8,6,18,1,8,17]{0,4,5,2,1,3:T(8,128)(2,1)} copy(bf16[8,6,18,1,8,17]{5,4,0,2,1,3:T(8,128)(2,1)S(1)} %reshape.38) | data formatting | bytes 470016 | tf_op jit(solution)/shard_map/conv_general_dilated | solution.py:48
  144.9 9.7 %broadcast_select_fusion.3 = f32[4,16,8,17,8]{4,2,3,1,0:T(8,128)} fusion(pred[8,17]{0,1:T(8,128)(4,1)S(1)} %copy-done.6, bf16[8,8,3,3,3]{1,0,4,3,2:T(8,128)(2,1)S(1)} %copy-done, bf16[8,6,18,1,7,2]{0,4,5,2,1,3:T(8,128)(2,1)S(1)} %slice.114, bf16[8,6,18,1,8,17]{0,4,5,2,1,3:T(8,128)(2,1)} %copy.155), kind=kOutput, calls=%fused_computation.38 | convolution fusion | flops 30938624 | bytes 541320 | tf_op jit(solution)/shard_map/conv_general_dilated | solution.py:48
  154.7 5.2 %copy.156 = f32[4,16,8,17,8]{3,2,4,1,0:T(8,128)S(1)} copy(f32[4,16,8,17,8]{4,2,3,1,0:T(8,128)} %broadcast_select_fusion.3) | data formatting | bytes 557056 | tf_op jit(solution)/shard_map/conv_general_dilated | solution.py:48
  160.5 7.5 %copy.164 = bf16[8,6,18,1,8,17]{0,4,5,2,1,3:T(8,128)(2,1)} copy(bf16[8,6,18,1,8,17]{5,4,0,2,1,3:T(8,128)(2,1)} %reshape.59) | data formatting | bytes 470016 | tf_op jit(solution)/shard_map/conv_general_dilated | solution.py:48
  169.1 9.7 %broadcast_select_fusion = f32[4,16,8,17,8]{4,2,3,1,0:T(8,128)} fusion(pred[8,17]{0,1:T(8,128)(4,1)S(1)} %copy-done.6, bf16[8,8,3,3,3]{1,0,4,3,2:T(8,128)(2,1)S(1)} %copy-done, bf16[8,6,18,1,7,2]{0,4,5,2,1,3:T(8,128)(2,1)S(1)} %slice.123, bf16[8,6,18,1,8,17]{0,4,5,2,1,3:T(8,128)(2,1)} %copy.164), kind=kOutput, calls=%fused_computation.35 | convolution fusion | flops 30938624 | bytes 541320 | tf_op jit(solution)/shard_map/conv_general_dilated | solution.py:48
  178.9 5.6 %copy.165 = f32[4,16,8,17,8]{3,2,4,1,0:T(8,128)S(1)} copy(f32[4,16,8,17,8]{4,2,3,1,0:T(8,128)} %broadcast_select_fusion) | data formatting | bytes 557056 | tf_op jit(solution)/shard_map/conv_general_dilated | solution.py:48
  185.1 7.5 %copy.161 = bf16[8,6,18,1,8,17]{0,4,5,2,1,3:T(8,128)(2,1)} copy(bf16[8,6,18,1,8,17]{5,4,0,2,1,3:T(8,128)(2,1)} %reshape.52) | data formatting | bytes 470016 | tf_op jit(solution)/shard_map/conv_general_dilated | solution.py:48
  193.7 9.7 %broadcast_select_fusion.1 = f32[4,16,8,17,8]{4,2,3,1,0:T(8,128)} fusion(pred[8,17]{0,1:T(8,128)(4,1)S(1)} %copy-done.6, bf16[8,8,3,3,3]{1,0,4,3,2:T(8,128)(2,1)S(1)} %copy-done, bf16[8,6,18,1,7,2]{0,4,5,2,1,3:T(8,128)(2,1)S(1)} %slice.120, bf16[8,6,18,1,8,17]{0,4,5,2,1,3:T(8,128)(2,1)} %copy.161), kind=kOutput, calls=%fused_computation.36 | convolution fusion | flops 30938624 | bytes 541320 | tf_op jit(solution)/shard_map/conv_general_dilated | solution.py:48
  203.5 5.2 %copy.162 = f32[4,16,8,17,8]{3,2,4,1,0:T(8,128)S(1)} copy(f32[4,16,8,17,8]{4,2,3,1,0:T(8,128)} %broadcast_select_fusion.1) | data formatting | bytes 557056 | tf_op jit(solution)/shard_map/conv_general_dilated | solution.py:48
  210.1 7.5 %copy.158 = bf16[8,6,18,1,8,17]{0,4,5,2,1,3:T(8,128)(2,1)} copy(bf16[8,6,18,1,8,17]{5,4,0,2,1,3:T(8,128)(2,1)} %reshape.45) | data formatting | bytes 470016 | tf_op jit(solution)/shard_map/conv_general_dilated | solution.py:48
  218.7 9.7 %broadcast_select_fusion.2 = f32[4,16,8,17,8]{4,2,3,1,0:T(8,128)} fusion(pred[8,17]{0,1:T(8,128)(4,1)S(1)} %copy-done.6, bf16[8,8,3,3,3]{1,0,4,3,2:T(8,128)(2,1)S(1)} %copy-done, bf16[8,6,18,1,7,2]{0,4,5,2,1,3:T(8,128)(2,1)S(1)} %slice.117, bf16[8,6,18,1,8,17]{0,4,5,2,1,3:T(8,128)(2,1)} %copy.158), kind=kOutput, calls=%fused_computation.37 | convolution fusion | flops 30938624 | bytes 541320 | tf_op jit(solution)/shard_map/conv_general_dilated | solution.py:48
  228.5 5.2 %copy.159 = f32[4,16,8,17,8]{3,2,4,1,0:T(8,128)S(1)} copy(f32[4,16,8,17,8]{4,2,3,1,0:T(8,128)} %broadcast_select_fusion.2) | data formatting | bytes 557056 | tf_op jit(solution)/shard_map/conv_general_dilated | solution.py:48
  238.3 5.8 %collective-permute-done.8 = bf16[8,16,1,128]{3,0,2,1:T(8,128)(2,1)S(1)} collective-permute-done((bf16[8,16,1,128]{3,0,2,1:T(8,128)(2,1)S(1)}, bf16[8,16,1,128]{3,0,2,1:T(8,128)(2,1)S(1)}, u32[]{:S(2)}, u32[]{:S(2)}) %collective-permute-start.8) | collective-permute-done | bytes 32800 | tf_op jit(solution)/shard_map/ppermute | solution.py:35
  244.1 3.2 %collective-permute-start.9 = (bf16[8,1,17,128]{3,0,2,1:T(8,128)(2,1)S(1)}, bf16[8,1,17,128]{3,0,2,1:T(8,128)(2,1)S(1)}, u32[]{:S(2)}, u32[]{:S(2)}) collective-permute-start(bf16[8,1,17,128]{3,0,2,1:T(8,128)(2,1)S(1)} %pad_maximum_fusion.1), channel_id=1, source_target_pairs={{0,16},{16,32},{32,48},{48,64},{64,80},{80,96},{96,112},{112,128},... | collective-permute-start | bytes 104456 | tf_op jit(solution)/shard_map/ppermute | solution.py:35
  247.2 5.6 %collective-permute-done.9 = bf16[8,1,17,128]{3,0,2,1:T(8,128)(2,1)S(1)} collective-permute-done((bf16[8,1,17,128]{3,0,2,1:T(8,128)(2,1)S(1)}, bf16[8,1,17,128]{3,0,2,1:T(8,128)(2,1)S(1)}, u32[]{:S(2)}, u32[]{:S(2)}) %collective-permute-start.9) | collective-permute-done | bytes 34848 | tf_op jit(solution)/shard_map/ppermute | solution.py:35
  253.4 5.7 %reshape.66 = bf16[8,17,17,1,8,18]{5,4,0,2,1,3:T(8,128)(2,1)} reshape(bf16[8,17,17,1,144]{4,0,2,1,3:T(8,128)(2,1)S(1)} %pad.16) | data formatting | bytes 1331712 | tf_op jit(solution)/shard_map/conv_general_dilated | solution.py:73
  259.1 18.6 %copy.167 = bf16[8,17,17,1,8,18]{0,4,5,2,1,3:T(8,128)(2,1)} copy(bf16[8,17,17,1,8,18]{5,4,0,2,1,3:T(8,128)(2,1)} %reshape.66) | data formatting | bytes 1331712 | tf_op jit(solution)/shard_map/conv_general_dilated | solution.py:73
  279.3 11.3 %fusion.50 = f32[8,8,8,9,16]{4,2,3,1,0:T(8,128)S(1)} fusion(bf16[16,8,3,3,3]{0,1,4,3,2:T(8,128)(2,1)S(1)} %copy-done.4, bf16[8,17,17,1,7,2]{0,4,5,2,1,3:T(8,128)(2,1)S(1)} %slice.125, bf16[8,17,17,1,8,18]{0,4,5,2,1,3:T(8,128)(2,1)} %copy.167, pred[8,9]{0,1:T(8,128)(4,1)S(1)} %copy-done.7), kind=kOutput, calls=%fused_computation.47 | convolution fusion | flops 34143744 | bytes 1032488 | tf_op jit(solution)/shard_map/conv_general_dilated | solution.py:73
  (103 shorter events, 58.7 us)
Async XLA Ops:
  0.0 144.9 %copy-start = (bf16[8,8,3,3,3]{1,0,4,3,2:T(8,128)(2,1)S(1)}, bf16[8,8,3,3,3]{1,0,4,3,2:T(8,128)(2,1)}, u32[]{:S(2)}) copy-start(bf16[8,8,3,3,3]{1,0,4,3,2:T(8,128)(2,1)} %param.10) | copy-start | bytes 10372
  13.3 9.2 %collective-permute-start = (bf16[1,16,128]{2,1,0:T(8,128)(2,1)S(1)}, bf16[1,16,128]{2,1,0:T(8,128)(2,1)S(1)}, u32[]{:S(2)}, u32[]{:S(2)}) collective-permute-start(bf16[1,16,128]{2,1,0:T(8,128)(2,1)S(1)} %slice_bitcast_fusion.16), channel_id=1, source_target_pairs={{0,16},{16,32},{32,48},{48,64},{64,80},{80,96},{96,112},{112,128},... | collective-permute-start | bytes 12296 | tf_op jit(solution)/shard_map/ppermute | solution.py:15
  18.5 7.1 %collective-permute-start.1 = (bf16[1,16,128]{2,1,0:T(8,128)(2,1)S(1)}, bf16[1,16,128]{2,1,0:T(8,128)(2,1)S(1)}, u32[]{:S(2)}, u32[]{:S(2)}) collective-permute-start(bf16[1,16,128]{2,1,0:T(8,128)(2,1)S(1)} %copy.172), channel_id=1, source_target_pairs={{16,0},{32,16},{48,32},{64,48},{80,64},{96,80},{112,96},{128,112},... | collective-permute-start | bytes 12296 | tf_op jit(solution)/shard_map/ppermute | solution.py:17
  25.6 7.7 %collective-permute-start.2 = (bf16[18,1,128]{2,1,0:T(2,128)(2,1)S(1)}, bf16[18,1,128]{2,1,0:T(2,128)(2,1)S(1)}, u32[]{:S(2)}, u32[]{:S(2)}) collective-permute-start(bf16[18,1,128]{2,1,0:T(2,128)(2,1)S(1)} %get-tuple-element.17), channel_id=1, source_target_pairs={{0,1},{1,2},{2,3},{3,4},{4,5},{5,6},{6,7},{7,8},{8,9},{9,10},{10,1... | collective-permute-start | bytes 13832 | tf_op jit(solution)/shard_map/ppermute | solution.py:15
  27.5 7.1 %collective-permute-start.3 = (bf16[18,1,128]{2,1,0:T(2,128)(2,1)S(1)}, bf16[18,1,128]{2,1,0:T(2,128)(2,1)S(1)}, u32[]{:S(2)}, u32[]{:S(2)}) collective-permute-start(bf16[18,1,128]{2,1,0:T(2,128)(2,1)S(1)} %get-tuple-element.18), channel_id=1, source_target_pairs={{1,0},{2,1},{3,2},{4,3},{5,4},{6,5},{7,6},{8,7},{9,8},{10,9},{11,1... | collective-permute-start | bytes 13832 | tf_op jit(solution)/shard_map/ppermute | solution.py:17
  36.1 8.8 %copy-start.5 = (bf16[8,1,3,3,3]{0,4,3,2,1:T(4,128)(2,1)S(1)}, bf16[8,1,3,3,3]{0,4,3,2,1:T(4,128)(2,1)}, u32[]{:S(2)}) copy-start(bf16[8,1,3,3,3]{0,4,3,2,1:T(4,128)(2,1)} %param.8) | copy-start | bytes 1300
  36.1 8.8 %copy-start.6 = (pred[8,17]{0,1:T(8,128)(4,1)S(1)}, pred[8,17]{0,1:T(8,128)(4,1)}, u32[]{:S(2)}) copy-start(pred[8,17]{0,1:T(8,128)(4,1)} %constant.41) | copy-start | bytes 412
  71.0 6.0 %copy-start.1 = (f32[8]{0:T(128)S(1)}, f32[8]{0:T(128)}, u32[]{:S(2)}) copy-start(f32[8]{0:T(128)} %param.9) | copy-start | bytes 100
  77.1 34.5 %collective-permute-start.4 = (bf16[8,1,16,128]{3,0,2,1:T(8,128)(2,1)S(1)}, bf16[8,1,16,128]{3,0,2,1:T(8,128)(2,1)S(1)}, u32[]{:S(2)}, u32[]{:S(2)}) collective-permute-start(bf16[8,1,16,128]{3,0,2,1:T(8,128)(2,1)S(1)} %slice.100), channel_id=1, source_target_pairs={{0,16},{16,32},{32,48},{48,64},{64,80},{80,96},{96,112},{112,128},... | collective-permute-start | bytes 98312 | tf_op jit(solution)/shard_map/ppermute | solution.py:15
  111.8 6.7 %collective-permute-start.5 = (bf16[8,1,16,128]{3,0,2,1:T(8,128)(2,1)S(1)}, bf16[8,1,16,128]{3,0,2,1:T(8,128)(2,1)S(1)}, u32[]{:S(2)}, u32[]{:S(2)}) collective-permute-start(bf16[8,1,16,128]{3,0,2,1:T(8,128)(2,1)S(1)} %slice.110), channel_id=1, source_target_pairs={{16,0},{32,16},{48,32},{64,48},{80,64},{96,80},{112,96},{128,112},... | collective-permute-start | bytes 98312 | tf_op jit(solution)/shard_map/ppermute | solution.py:17
  118.6 7.7 %collective-permute-start.6 = (bf16[8,18,1,128]{3,0,2,1:T(8,128)(2,1)S(1)}, bf16[8,18,1,128]{3,0,2,1:T(8,128)(2,1)S(1)}, u32[]{:S(2)}, u32[]{:S(2)}) collective-permute-start(bf16[8,18,1,128]{3,0,2,1:T(8,128)(2,1)S(1)} %get-tuple-element.11), channel_id=1, source_target_pairs={{0,1},{1,2},{2,3},{3,4},{4,5},{5,6},{6,7},{7,8},{8,9},{9,10},{10,1... | collective-permute-start | bytes 110600 | tf_op jit(solution)/shard_map/ppermute | solution.py:15
  120.5 7.4 %collective-permute-start.7 = (bf16[8,18,1,128]{3,0,2,1:T(8,128)(2,1)S(1)}, bf16[8,18,1,128]{3,0,2,1:T(8,128)(2,1)S(1)}, u32[]{:S(2)}, u32[]{:S(2)}) collective-permute-start(bf16[8,18,1,128]{3,0,2,1:T(8,128)(2,1)S(1)} %get-tuple-element.12), channel_id=1, source_target_pairs={{1,0},{2,1},{3,2},{4,3},{5,4},{6,5},{7,6},{8,7},{9,8},{10,9},{11,1... | collective-permute-start | bytes 110600 | tf_op jit(solution)/shard_map/ppermute | solution.py:17
  228.5 6.6 %copy-start.2 = (f32[8]{0:T(128)S(1)}, f32[8]{0:T(128)}, u32[]{:S(2)}) copy-start(f32[8]{0:T(128)} %param.11) | copy-start | bytes 100
  236.3 7.7 %collective-permute-start.8 = (bf16[8,16,1,128]{3,0,2,1:T(8,128)(2,1)S(1)}, bf16[8,16,1,128]{3,0,2,1:T(8,128)(2,1)S(1)}, u32[]{:S(2)}, u32[]{:S(2)}) collective-permute-start(bf16[8,16,1,128]{3,0,2,1:T(8,128)(2,1)S(1)} %pad_maximum_fusion.5), channel_id=1, source_target_pairs={{0,1},{1,2},{2,3},{3,4},{4,5},{5,6},{6,7},{7,8},{8,9},{9,10},{10,1... | collective-permute-start | bytes 98312 | tf_op jit(solution)/shard_map/ppermute | solution.py:35
  244.1 8.8 %collective-permute-start.9 = (bf16[8,1,17,128]{3,0,2,1:T(8,128)(2,1)S(1)}, bf16[8,1,17,128]{3,0,2,1:T(8,128)(2,1)S(1)}, u32[]{:S(2)}, u32[]{:S(2)}) collective-permute-start(bf16[8,1,17,128]{3,0,2,1:T(8,128)(2,1)S(1)} %pad_maximum_fusion.1), channel_id=1, source_target_pairs={{0,16},{16,32},{32,48},{48,64},{64,80},{80,96},{96,112},{112,128},... | collective-permute-start | bytes 104456 | tf_op jit(solution)/shard_map/ppermute | solution.py:35
  259.1 20.3 %copy-start.4 = (bf16[16,8,3,3,3]{0,1,4,3,2:T(8,128)(2,1)S(1)}, bf16[16,8,3,3,3]{0,1,4,3,2:T(8,128)(2,1)}, u32[]{:S(2)}) copy-start(bf16[16,8,3,3,3]{0,1,4,3,2:T(8,128)(2,1)} %param.12) | copy-start | bytes 20740
  259.1 20.3 %copy-start.7 = (pred[8,9]{0,1:T(8,128)(4,1)S(1)}, pred[8,9]{0,1:T(8,128)(4,1)}, u32[]{:S(2)}) copy-start(pred[8,9]{0,1:T(8,128)(4,1)} %constant.40) | copy-start | bytes 220
  291.1 1.0 copy-start.3
where the time goes:
time: 297 us; the launch traced here: 293 us
  local copies, waits for them, and re-layouts  131 us (44%)
  matrix products  86 us (29%)
  starting transfers between devices  38.5 us (13%)
  waiting for transfers between devices  19 us (6%)
  blocking collectives  10.6 us (4%)
  other arithmetic  7.4 us (2%)
    conv_general_dilated x40, local copies, waits for them, and re-layouts, conv_layer(): lax.conv_general_dilated(section[None], kernel, (1, 1, 1), ((0, 0), (0, 0...  101 us
    conv_general_dilated x8, matrix products, conv_layer(): lax.conv_general_dilated(section[None], kernel, (1, 1, 1), ((0, 0), (0, 0...  74.6 us
    conv_general_dilated x5, local copies, waits for them, and re-layouts, body(): lax.conv_general_dilated(extended[None], kernel_three, (2, 2, 2), ((0, 0)...  26.5 us
    ppermute x4, starting transfers between devices, extended_2(): lax.ppermute(head, axis, [((i + 1) % count, i) for i in range(ends)])  18.3 us
    ppermute x4, starting transfers between devices, extended_2(): lax.ppermute(tail, axis, [(i, (i + 1) % count) for i in range(ends)])  15.1 us
    ppermute x2, waiting for transfers between devices, from_behind(): return lax.ppermute(shard, axis, pairs)  11.5 us
    conv_general_dilated x1, matrix products, body(): lax.conv_general_dilated(extended[None], kernel_three, (2, 2, 2), ((0, 0)...  11.3 us
    all_to_all x1, blocking collectives, body(): lax.all_to_all(sky_cube.astype(jnp.bfloat16), 'tile', split_axis=1, conca...  10.6 us
  transfers between devices with their start and end apart: 10, of which 6 were waited for; matrix products, arithmetic and copies ran while one was open for 10% of the time, Pallas kernels for 0%

commit v1 on v0

--- a/solution.py
+++ b/solution.py
@@ -59,8 +59,14 @@
 
 
 def body(sky_cube, kernel_one, bias_one, kernel_two, bias_two, kernel_three, bias_three):
-    slab = lax.all_to_all(
-        sky_cube.astype(jnp.bfloat16), "tile", split_axis=1, concat_axis=0, tiled=True
+    slab = jnp.concatenate(
+        lax.all_to_all(
+            jnp.stack(jnp.split(sky_cube.astype(jnp.bfloat16), lax.axis_size("tile"), axis=1)),
+            "tile",
+            0,
+            0,
+        ),
+        axis=0,
     )
     widened = extended_2(slab, (("freq", 0), ("tile", 1)), 1)
     layer_one = conv_layer(widened[None], kernel_one, bias_one)

time: 297 us -> 295 us (level)
  transfers between devices with their start and end apart: 10 -> 10, of which waited for: 6 -> 6; matrix products, arithmetic and copies ran while one was open for 10% -> 11% of each run, Pallas kernels for 0% -> 0%
where the time goes in v1:
time: 295 us; the launch traced here: 292 us
  local copies, waits for them, and re-layouts  130 us (44%)
  matrix products  86.2 us (29%)
  starting transfers between devices  38.5 us (13%)
  waiting for transfers between devices  19 us (6%)
  blocking collectives  10.6 us (4%)
  other arithmetic  6.38 us (2%)
    conv_general_dilated x40, local copies, waits for them, and re-layouts, conv_layer(): lax.conv_general_dilated(section[None], kernel, (1, 1, 1), ((0, 0), (0, 0...  101 us
    conv_general_dilated x8, matrix products, conv_layer(): lax.conv_general_dilated(section[None], kernel, (1, 1, 1), ((0, 0), (0, 0...  74.9 us
    conv_general_dilated x5, local copies, waits for them, and re-layouts, body(): lax.conv_general_dilated(extended[None], kernel_three, (2, 2, 2), ((0, 0)...  26.5 us
    ppermute x4, starting transfers between devices, extended_2(): lax.ppermute(head, axis, [((i + 1) % count, i) for i in range(ends)])  18.3 us
    ppermute x4, starting transfers between devices, extended_2(): lax.ppermute(tail, axis, [(i, (i + 1) % count) for i in range(ends)])  15 us
    ppermute x2, waiting for transfers between devices, from_behind(): return lax.ppermute(shard, axis, pairs)  11.5 us
    conv_general_dilated x1, matrix products, body(): lax.conv_general_dilated(extended[None], kernel_three, (2, 2, 2), ((0, 0)...  11.3 us
    all_to_all x1, blocking collectives, body(): lax.all_to_all(jnp.stack(jnp.split(sky_cube.astype(jnp.bfloat16), lax.axi...  10.6 us
  transfers between devices with their start and end apart: 10, of which 6 were waited for; matrix products, arithmetic and copies ran while one was open for 11% of the time, Pallas kernels for 0%

profile of v1, /device:TPU:34, one launch (start us, length us, event | category | flops | bytes accessed | tf_op | source)
XLA Modules:
  0.0 291.6 jit_solution(7645015074398607450)
XLA Ops:
  1.1 10.6 %all_to_all.5 = bf16[16,1,16,128]{3,2,1,0:T(8,128)(2,1)S(1)} all-to-all(bf16[16,1,16,128]{3,2,1,0:T(8,128)(2,1)S(1)} %constant_dynamic-update-slice_fusion), channel_id=1, replica_groups=mesh['freq'=16,'tile'=16] {'tile'}, dimensions={0} | all-to-all | bytes 131072 | tf_op jit(solution)/shard_map/all_to_all | solution.py:63
  11.7 5.2 %collective-permute-start = (bf16[1,16,128]{2,1,0:T(8,128)(2,1)S(1)}, bf16[1,16,128]{2,1,0:T(8,128)(2,1)S(1)}, u32[]{:S(2)}, u32[]{:S(2)}) collective-permute-start(bf16[1,16,128]{2,1,0:T(8,128)(2,1)S(1)} %get-tuple-element.19), channel_id=1, source_target_pairs={{0,16},{16,32},{32,48},{48,64},{64,80},{80,96},{96,112},{112,128},... | collective-permute-start | bytes 12296 | tf_op jit(solution)/shard_map/ppermute | solution.py:15
  16.9 4.0 %collective-permute-start.1 = (bf16[1,16,128]{2,1,0:T(8,128)(2,1)S(1)}, bf16[1,16,128]{2,1,0:T(8,128)(2,1)S(1)}, u32[]{:S(2)}, u32[]{:S(2)}) collective-permute-start(bf16[1,16,128]{2,1,0:T(8,128)(2,1)S(1)} %get-tuple-element.20), channel_id=1, source_target_pairs={{16,0},{32,16},{48,32},{64,48},{80,64},{96,80},{112,96},{128,112},... | collective-permute-start | bytes 12296 | tf_op jit(solution)/shard_map/ppermute | solution.py:17
  25.9 5.8 %collective-permute-start.3 = (bf16[18,1,128]{2,1,0:T(2,128)(2,1)S(1)}, bf16[18,1,128]{2,1,0:T(2,128)(2,1)S(1)}, u32[]{:S(2)}, u32[]{:S(2)}) collective-permute-start(bf16[18,1,128]{2,1,0:T(2,128)(2,1)S(1)} %get-tuple-element.18), channel_id=1, source_target_pairs={{1,0},{2,1},{3,2},{4,3},{5,4},{6,5},{7,6},{8,7},{9,8},{10,9},{11,1... | collective-permute-start | bytes 13832 | tf_op jit(solution)/shard_map/ppermute | solution.py:17
  43.3 8.7 %broadcast_select_fusion.4 = f32[4,16,8,17,8]{4,2,3,1,0:T(8,128)} fusion(pred[8,17]{0,1:T(8,128)(4,1)S(1)} %copy-done.6, bf16[1,6,18,8,19]{3,0,4,2,1:T(2,128)(2,1)S(1)} %copy.110, bf16[8,1,3,3,3]{0,4,3,2,1:T(4,128)(2,1)S(1)} %copy-done.5), kind=kOutput, calls=%fused_computation.39 | convolution fusion | flops 3829760 | bytes 311928 | tf_op jit(solution)/shard_map/conv_general_dilated | solution.py:48
  52.0 8.8 %broadcast_select_fusion.5 = f32[4,16,8,17,8]{4,2,3,1,0:T(8,128)} fusion(pred[8,17]{0,1:T(8,128)(4,1)S(1)} %copy-done.6, bf16[1,6,18,8,19]{3,0,4,2,1:T(2,128)(2,1)S(1)} %copy.107, bf16[8,1,3,3,3]{0,4,3,2,1:T(4,128)(2,1)S(1)} %copy-done.5), kind=kOutput, calls=%fused_computation.40 | convolution fusion | flops 3829760 | bytes 311928 | tf_op jit(solution)/shard_map/conv_general_dilated | solution.py:48
  60.8 8.8 %broadcast_select_fusion.7 = f32[4,16,8,17,8]{4,2,3,1,0:T(8,128)} fusion(pred[8,17]{0,1:T(8,128)(4,1)S(1)} %copy-done.6, bf16[1,6,18,8,19]{3,0,4,2,1:T(2,128)(2,1)S(1)} %copy.101, bf16[8,1,3,3,3]{0,4,3,2,1:T(4,128)(2,1)S(1)} %copy-done.5), kind=kOutput, calls=%fused_computation.42 | convolution fusion | flops 3829760 | bytes 311928 | tf_op jit(solution)/shard_map/conv_general_dilated | solution.py:48
  69.5 5.4 %copy.103 = f32[4,16,8,17,8]{3,2,4,1,0:T(8,128)S(1)} copy(f32[4,16,8,17,8]{4,2,3,1,0:T(8,128)} %broadcast_select_fusion.7) | data formatting | bytes 557056 | tf_op jit(solution)/shard_map/conv_general_dilated | solution.py:48
  75.6 6.0 %collective-permute-start.4 = (bf16[8,1,16,128]{3,0,2,1:T(8,128)(2,1)S(1)}, bf16[8,1,16,128]{3,0,2,1:T(8,128)(2,1)S(1)}, u32[]{:S(2)}, u32[]{:S(2)}) collective-permute-start(bf16[8,1,16,128]{3,0,2,1:T(8,128)(2,1)S(1)} %slice.103), channel_id=1, source_target_pairs={{0,16},{16,32},{32,48},{48,64},{64,80},{80,96},{96,112},{112,128},... | collective-permute-start | bytes 98312 | tf_op jit(solution)/shard_map/ppermute | solution.py:15
  81.7 9.6 %broadcast_select_fusion.6 = f32[4,16,8,17,8]{4,2,3,1,0:T(8,128)} fusion(pred[8,17]{0,1:T(8,128)(4,1)S(1)} %copy-done.6, bf16[1,6,18,8,19]{3,0,4,2,1:T(2,128)(2,1)} %copy.104, bf16[8,1,3,3,3]{0,4,3,2,1:T(4,128)(2,1)S(1)} %copy-done.5), kind=kOutput, calls=%fused_computation.41 | convolution fusion | flops 3829760 | bytes 311928 | tf_op jit(solution)/shard_map/conv_general_dilated | solution.py:48
  91.3 5.2 %copy.112 = f32[4,16,8,17,8]{3,2,4,1,0:T(8,128)S(1)} copy(f32[4,16,8,17,8]{4,2,3,1,0:T(8,128)} %broadcast_select_fusion.4) | data formatting | bytes 557056 | tf_op jit(solution)/shard_map/conv_general_dilated | solution.py:48
  97.8 5.2 %copy.109 = f32[4,16,8,17,8]{3,2,4,1,0:T(8,128)S(1)} copy(f32[4,16,8,17,8]{4,2,3,1,0:T(8,128)} %broadcast_select_fusion.5) | data formatting | bytes 557056 | tf_op jit(solution)/shard_map/conv_general_dilated | solution.py:48
  104.4 5.2 %copy.106 = f32[4,16,8,17,8]{3,2,4,1,0:T(8,128)S(1)} copy(f32[4,16,8,17,8]{4,2,3,1,0:T(8,128)} %broadcast_select_fusion.6) | data formatting | bytes 557056 | tf_op jit(solution)/shard_map/conv_general_dilated | solution.py:48
  119.0 5.8 %collective-permute-start.7 = (bf16[8,18,1,128]{3,0,2,1:T(8,128)(2,1)S(1)}, bf16[8,18,1,128]{3,0,2,1:T(8,128)(2,1)S(1)}, u32[]{:S(2)}, u32[]{:S(2)}) collective-permute-start(bf16[8,18,1,128]{3,0,2,1:T(8,128)(2,1)S(1)} %get-tuple-element.12), channel_id=1, source_target_pairs={{1,0},{2,1},{3,2},{4,3},{5,4},{6,5},{7,6},{8,7},{9,8},{10,9},{11,1... | collective-permute-start | bytes 110600 | tf_op jit(solution)/shard_map/ppermute | solution.py:17
  135.6 6.6 %copy.114 = bf16[8,6,18,1,8,17]{0,4,5,2,1,3:T(8,128)(2,1)} copy(bf16[8,6,18,1,8,17]{5,4,0,2,1,3:T(8,128)(2,1)S(1)} %reshape.39) | data formatting | bytes 470016 | tf_op jit(solution)/shard_map/conv_general_dilated | solution.py:48
  143.4 9.8 %broadcast_select_fusion.3 = f32[4,16,8,17,8]{4,2,3,1,0:T(8,128)} fusion(pred[8,17]{0,1:T(8,128)(4,1)S(1)} %copy-done.6, bf16[8,8,3,3,3]{1,0,4,3,2:T(8,128)(2,1)S(1)} %copy-done, bf16[8,6,18,1,7,2]{0,4,5,2,1,3:T(8,128)(2,1)S(1)} %slice.117, bf16[8,6,18,1,8,17]{0,4,5,2,1,3:T(8,128)(2,1)} %copy.114), kind=kOutput, calls=%fused_computation.38 | convolution fusion | flops 30938624 | bytes 541320 | tf_op jit(solution)/shard_map/conv_general_dilated | solution.py:48
  153.2 5.2 %copy.115 = f32[4,16,8,17,8]{3,2,4,1,0:T(8,128)S(1)} copy(f32[4,16,8,17,8]{4,2,3,1,0:T(8,128)} %broadcast_select_fusion.3) | data formatting | bytes 557056 | tf_op jit(solution)/shard_map/conv_general_dilated | solution.py:48
  158.9 7.5 %copy.123 = bf16[8,6,18,1,8,17]{0,4,5,2,1,3:T(8,128)(2,1)} copy(bf16[8,6,18,1,8,17]{5,4,0,2,1,3:T(8,128)(2,1)} %reshape.60) | data formatting | bytes 470016 | tf_op jit(solution)/shard_map/conv_general_dilated | solution.py:48
  167.6 9.8 %broadcast_select_fusion = f32[4,16,8,17,8]{4,2,3,1,0:T(8,128)} fusion(pred[8,17]{0,1:T(8,128)(4,1)S(1)} %copy-done.6, bf16[8,8,3,3,3]{1,0,4,3,2:T(8,128)(2,1)S(1)} %copy-done, bf16[8,6,18,1,7,2]{0,4,5,2,1,3:T(8,128)(2,1)S(1)} %slice.126, bf16[8,6,18,1,8,17]{0,4,5,2,1,3:T(8,128)(2,1)} %copy.123), kind=kOutput, calls=%fused_computation.35 | convolution fusion | flops 30938624 | bytes 541320 | tf_op jit(solution)/shard_map/conv_general_dilated | solution.py:48
  177.4 5.6 %copy.124 = f32[4,16,8,17,8]{3,2,4,1,0:T(8,128)S(1)} copy(f32[4,16,8,17,8]{4,2,3,1,0:T(8,128)} %broadcast_select_fusion) | data formatting | bytes 557056 | tf_op jit(solution)/shard_map/conv_general_dilated | solution.py:48
  183.5 7.5 %copy.120 = bf16[8,6,18,1,8,17]{0,4,5,2,1,3:T(8,128)(2,1)} copy(bf16[8,6,18,1,8,17]{5,4,0,2,1,3:T(8,128)(2,1)} %reshape.53) | data formatting | bytes 470016 | tf_op jit(solution)/shard_map/conv_general_dilated | solution.py:48
  192.2 9.8 %broadcast_select_fusion.1 = f32[4,16,8,17,8]{4,2,3,1,0:T(8,128)} fusion(pred[8,17]{0,1:T(8,128)(4,1)S(1)} %copy-done.6, bf16[8,8,3,3,3]{1,0,4,3,2:T(8,128)(2,1)S(1)} %copy-done, bf16[8,6,18,1,7,2]{0,4,5,2,1,3:T(8,128)(2,1)S(1)} %slice.123, bf16[8,6,18,1,8,17]{0,4,5,2,1,3:T(8,128)(2,1)} %copy.120), kind=kOutput, calls=%fused_computation.36 | convolution fusion | flops 30938624 | bytes 541320 | tf_op jit(solution)/shard_map/conv_general_dilated | solution.py:48
  202.0 5.2 %copy.121 = f32[4,16,8,17,8]{3,2,4,1,0:T(8,128)S(1)} copy(f32[4,16,8,17,8]{4,2,3,1,0:T(8,128)} %broadcast_select_fusion.1) | data formatting | bytes 557056 | tf_op jit(solution)/shard_map/conv_general_dilated | solution.py:48
  208.6 7.5 %copy.117 = bf16[8,6,18,1,8,17]{0,4,5,2,1,3:T(8,128)(2,1)} copy(bf16[8,6,18,1,8,17]{5,4,0,2,1,3:T(8,128)(2,1)} %reshape.46) | data formatting | bytes 470016 | tf_op jit(solution)/shard_map/conv_general_dilated | solution.py:48
  217.2 9.8 %broadcast_select_fusion.2 = f32[4,16,8,17,8]{4,2,3,1,0:T(8,128)} fusion(pred[8,17]{0,1:T(8,128)(4,1)S(1)} %copy-done.6, bf16[8,8,3,3,3]{1,0,4,3,2:T(8,128)(2,1)S(1)} %copy-done, bf16[8,6,18,1,7,2]{0,4,5,2,1,3:T(8,128)(2,1)S(1)} %slice.120, bf16[8,6,18,1,8,17]{0,4,5,2,1,3:T(8,128)(2,1)} %copy.117), kind=kOutput, calls=%fused_computation.37 | convolution fusion | flops 30938624 | bytes 541320 | tf_op jit(solution)/shard_map/conv_general_dilated | solution.py:48
  227.0 5.2 %copy.118 = f32[4,16,8,17,8]{3,2,4,1,0:T(8,128)S(1)} copy(f32[4,16,8,17,8]{4,2,3,1,0:T(8,128)} %broadcast_select_fusion.2) | data formatting | bytes 557056 | tf_op jit(solution)/shard_map/conv_general_dilated | solution.py:48
  236.8 5.8 %collective-permute-done.8 = bf16[8,16,1,128]{3,0,2,1:T(8,128)(2,1)S(1)} collective-permute-done((bf16[8,16,1,128]{3,0,2,1:T(8,128)(2,1)S(1)}, bf16[8,16,1,128]{3,0,2,1:T(8,128)(2,1)S(1)}, u32[]{:S(2)}, u32[]{:S(2)}) %collective-permute-start.8) | collective-permute-done | bytes 32800 | tf_op jit(solution)/shard_map/ppermute | solution.py:35
  242.6 3.2 %collective-permute-start.9 = (bf16[8,1,17,128]{3,0,2,1:T(8,128)(2,1)S(1)}, bf16[8,1,17,128]{3,0,2,1:T(8,128)(2,1)S(1)}, u32[]{:S(2)}, u32[]{:S(2)}) collective-permute-start(bf16[8,1,17,128]{3,0,2,1:T(8,128)(2,1)S(1)} %pad_maximum_fusion.1), channel_id=1, source_target_pairs={{0,16},{16,32},{32,48},{48,64},{64,80},{80,96},{96,112},{112,128},... | collective-permute-start | bytes 104456 | tf_op jit(solution)/shard_map/ppermute | solution.py:35
  245.8 5.7 %collective-permute-done.9 = bf16[8,1,17,128]{3,0,2,1:T(8,128)(2,1)S(1)} collective-permute-done((bf16[8,1,17,128]{3,0,2,1:T(8,128)(2,1)S(1)}, bf16[8,1,17,128]{3,0,2,1:T(8,128)(2,1)S(1)}, u32[]{:S(2)}, u32[]{:S(2)}) %collective-permute-start.9) | collective-permute-done | bytes 34848 | tf_op jit(solution)/shard_map/ppermute | solution.py:35
  251.9 5.7 %reshape.67 = bf16[8,17,17,1,8,18]{5,4,0,2,1,3:T(8,128)(2,1)} reshape(bf16[8,17,17,1,144]{4,0,2,1,3:T(8,128)(2,1)S(1)} %pad.16) | data formatting | bytes 1331712 | tf_op jit(solution)/shard_map/conv_general_dilated | solution.py:79
  257.6 18.6 %copy.126 = bf16[8,17,17,1,8,18]{0,4,5,2,1,3:T(8,128)(2,1)} copy(bf16[8,17,17,1,8,18]{5,4,0,2,1,3:T(8,128)(2,1)} %reshape.67) | data formatting | bytes 1331712 | tf_op jit(solution)/shard_map/conv_general_dilated | solution.py:79
  277.8 11.3 %fusion.50 = f32[8,8,8,9,16]{4,2,3,1,0:T(8,128)S(1)} fusion(bf16[16,8,3,3,3]{0,1,4,3,2:T(8,128)(2,1)S(1)} %copy-done.4, bf16[8,17,17,1,7,2]{0,4,5,2,1,3:T(8,128)(2,1)S(1)} %slice.128, bf16[8,17,17,1,8,18]{0,4,5,2,1,3:T(8,128)(2,1)} %copy.126, pred[8,9]{0,1:T(8,128)(4,1)S(1)} %copy-done.7), kind=kOutput, calls=%fused_computation.47 | convolution fusion | flops 34143744 | bytes 1032488 | tf_op jit(solution)/shard_map/conv_general_dilated | solution.py:79
  (111 shorter events, 57.1 us)
Async XLA Ops:
  0.0 143.4 %copy-start = (bf16[8,8,3,3,3]{1,0,4,3,2:T(8,128)(2,1)S(1)}, bf16[8,8,3,3,3]{1,0,4,3,2:T(8,128)(2,1)}, u32[]{:S(2)}) copy-start(bf16[8,8,3,3,3]{1,0,4,3,2:T(8,128)(2,1)} %param.10) | copy-start | bytes 10372
  11.7 9.2 %collective-permute-start = (bf16[1,16,128]{2,1,0:T(8,128)(2,1)S(1)}, bf16[1,16,128]{2,1,0:T(8,128)(2,1)S(1)}, u32[]{:S(2)}, u32[]{:S(2)}) collective-permute-start(bf16[1,16,128]{2,1,0:T(8,128)(2,1)S(1)} %get-tuple-element.19), channel_id=1, source_target_pairs={{0,16},{16,32},{32,48},{48,64},{64,80},{80,96},{96,112},{112,128},... | collective-permute-start | bytes 12296 | tf_op jit(solution)/shard_map/ppermute | solution.py:15
  16.9 7.1 %collective-permute-start.1 = (bf16[1,16,128]{2,1,0:T(8,128)(2,1)S(1)}, bf16[1,16,128]{2,1,0:T(8,128)(2,1)S(1)}, u32[]{:S(2)}, u32[]{:S(2)}) collective-permute-start(bf16[1,16,128]{2,1,0:T(8,128)(2,1)S(1)} %get-tuple-element.20), channel_id=1, source_target_pairs={{16,0},{32,16},{48,32},{64,48},{80,64},{96,80},{112,96},{128,112},... | collective-permute-start | bytes 12296 | tf_op jit(solution)/shard_map/ppermute | solution.py:17
  24.0 7.7 %collective-permute-start.2 = (bf16[18,1,128]{2,1,0:T(2,128)(2,1)S(1)}, bf16[18,1,128]{2,1,0:T(2,128)(2,1)S(1)}, u32[]{:S(2)}, u32[]{:S(2)}) collective-permute-start(bf16[18,1,128]{2,1,0:T(2,128)(2,1)S(1)} %get-tuple-element.17), channel_id=1, source_target_pairs={{0,1},{1,2},{2,3},{3,4},{4,5},{5,6},{6,7},{7,8},{8,9},{9,10},{10,1... | collective-permute-start | bytes 13832 | tf_op jit(solution)/shard_map/ppermute | solution.py:15
  25.9 7.1 %collective-permute-start.3 = (bf16[18,1,128]{2,1,0:T(2,128)(2,1)S(1)}, bf16[18,1,128]{2,1,0:T(2,128)(2,1)S(1)}, u32[]{:S(2)}, u32[]{:S(2)}) collective-permute-start(bf16[18,1,128]{2,1,0:T(2,128)(2,1)S(1)} %get-tuple-element.18), channel_id=1, source_target_pairs={{1,0},{2,1},{3,2},{4,3},{5,4},{6,5},{7,6},{8,7},{9,8},{10,9},{11,1... | collective-permute-start | bytes 13832 | tf_op jit(solution)/shard_map/ppermute | solution.py:17
  34.5 8.8 %copy-start.5 = (bf16[8,1,3,3,3]{0,4,3,2,1:T(4,128)(2,1)S(1)}, bf16[8,1,3,3,3]{0,4,3,2,1:T(4,128)(2,1)}, u32[]{:S(2)}) copy-start(bf16[8,1,3,3,3]{0,4,3,2,1:T(4,128)(2,1)} %param.8) | copy-start | bytes 1300
  34.5 8.8 %copy-start.6 = (pred[8,17]{0,1:T(8,128)(4,1)S(1)}, pred[8,17]{0,1:T(8,128)(4,1)}, u32[]{:S(2)}) copy-start(pred[8,17]{0,1:T(8,128)(4,1)} %constant.41) | copy-start | bytes 412
  69.5 6.0 %copy-start.1 = (f32[8]{0:T(128)S(1)}, f32[8]{0:T(128)}, u32[]{:S(2)}) copy-start(f32[8]{0:T(128)} %param.9) | copy-start | bytes 100
  75.6 34.5 %collective-permute-start.4 = (bf16[8,1,16,128]{3,0,2,1:T(8,128)(2,1)S(1)}, bf16[8,1,16,128]{3,0,2,1:T(8,128)(2,1)S(1)}, u32[]{:S(2)}, u32[]{:S(2)}) collective-permute-start(bf16[8,1,16,128]{3,0,2,1:T(8,128)(2,1)S(1)} %slice.103), channel_id=1, source_target_pairs={{0,16},{16,32},{32,48},{48,64},{64,80},{80,96},{96,112},{112,128},... | collective-permute-start | bytes 98312 | tf_op jit(solution)/shard_map/ppermute | solution.py:15
  110.3 6.7 %collective-permute-start.5 = (bf16[8,1,16,128]{3,0,2,1:T(8,128)(2,1)S(1)}, bf16[8,1,16,128]{3,0,2,1:T(8,128)(2,1)S(1)}, u32[]{:S(2)}, u32[]{:S(2)}) collective-permute-start(bf16[8,1,16,128]{3,0,2,1:T(8,128)(2,1)S(1)} %slice.113), channel_id=1, source_target_pairs={{16,0},{32,16},{48,32},{64,48},{80,64},{96,80},{112,96},{128,112},... | collective-permute-start | bytes 98312 | tf_op jit(solution)/shard_map/ppermute | solution.py:17
  117.1 7.7 %collective-permute-start.6 = (bf16[8,18,1,128]{3,0,2,1:T(8,128)(2,1)S(1)}, bf16[8,18,1,128]{3,0,2,1:T(8,128)(2,1)S(1)}, u32[]{:S(2)}, u32[]{:S(2)}) collective-permute-start(bf16[8,18,1,128]{3,0,2,1:T(8,128)(2,1)S(1)} %get-tuple-element.11), channel_id=1, source_target_pairs={{0,1},{1,2},{2,3},{3,4},{4,5},{5,6},{6,7},{7,8},{8,9},{9,10},{10,1... | collective-permute-start | bytes 110600 | tf_op jit(solution)/shard_map/ppermute | solution.py:15
  119.0 7.4 %collective-permute-start.7 = (bf16[8,18,1,128]{3,0,2,1:T(8,128)(2,1)S(1)}, bf16[8,18,1,128]{3,0,2,1:T(8,128)(2,1)S(1)}, u32[]{:S(2)}, u32[]{:S(2)}) collective-permute-start(bf16[8,18,1,128]{3,0,2,1:T(8,128)(2,1)S(1)} %get-tuple-element.12), channel_id=1, source_target_pairs={{1,0},{2,1},{3,2},{4,3},{5,4},{6,5},{7,6},{8,7},{9,8},{10,9},{11,1... | collective-permute-start | bytes 110600 | tf_op jit(solution)/shard_map/ppermute | solution.py:17
  227.0 6.6 %copy-start.2 = (f32[8]{0:T(128)S(1)}, f32[8]{0:T(128)}, u32[]{:S(2)}) copy-start(f32[8]{0:T(128)} %param.11) | copy-start | bytes 100
  234.8 7.7 %collective-permute-start.8 = (bf16[8,16,1,128]{3,0,2,1:T(8,128)(2,1)S(1)}, bf16[8,16,1,128]{3,0,2,1:T(8,128)(2,1)S(1)}, u32[]{:S(2)}, u32[]{:S(2)}) collective-permute-start(bf16[8,16,1,128]{3,0,2,1:T(8,128)(2,1)S(1)} %pad_maximum_fusion.5), channel_id=1, source_target_pairs={{0,1},{1,2},{2,3},{3,4},{4,5},{5,6},{6,7},{7,8},{8,9},{9,10},{10,1... | collective-permute-start | bytes 98312 | tf_op jit(solution)/shard_map/ppermute | solution.py:35
  242.6 8.8 %collective-permute-start.9 = (bf16[8,1,17,128]{3,0,2,1:T(8,128)(2,1)S(1)}, bf16[8,1,17,128]{3,0,2,1:T(8,128)(2,1)S(1)}, u32[]{:S(2)}, u32[]{:S(2)}) collective-permute-start(bf16[8,1,17,128]{3,0,2,1:T(8,128)(2,1)S(1)} %pad_maximum_fusion.1), channel_id=1, source_target_pairs={{0,16},{16,32},{32,48},{48,64},{64,80},{80,96},{96,112},{112,128},... | collective-permute-start | bytes 104456 | tf_op jit(solution)/shard_map/ppermute | solution.py:35
  257.6 20.2 %copy-start.4 = (bf16[16,8,3,3,3]{0,1,4,3,2:T(8,128)(2,1)S(1)}, bf16[16,8,3,3,3]{0,1,4,3,2:T(8,128)(2,1)}, u32[]{:S(2)}) copy-start(bf16[16,8,3,3,3]{0,1,4,3,2:T(8,128)(2,1)} %param.12) | copy-start | bytes 20740
  257.6 20.2 %copy-start.7 = (pred[8,9]{0,1:T(8,128)(4,1)S(1)}, pred[8,9]{0,1:T(8,128)(4,1)}, u32[]{:S(2)}) copy-start(pred[8,9]{0,1:T(8,128)(4,1)} %constant.40) | copy-start | bytes 220
  289.6 1.0 copy-start.3
